TPU v7x, 256 devices: a whole 4x4x8 slice. The times are simulated.
256 devices in a mesh: dp: 16 (over z, core), mp: 16 (over y, x).
Axes of the slice: x: 4, y: 4, z: 8, core: 2. Of those that a mesh axis runs over, the one named last changes fastest.
Arguments:
- candidates: bfloat16 [4096, 4096], P('dp', 'mp'), may hold values from -6 to 6
- hold_gate: bfloat16 [4096, 8192], P(None, 'mp'), may hold values from -0.09375 to 0.09375
- hold_up: bfloat16 [4096, 8192], P(None, 'mp'), may hold values from -0.09375 to 0.09375
- probe: float32 [8192], P('mp'), as said below
- chosen: int32 [16, 192], replicated, may hold values from 0 to 4095, as said below
- counts: int32 [16], replicated, may hold values from 24 to 192, as said below
- gate_w: bfloat16 [4096, 14336], P('dp', 'mp'), may hold values from -0.09375 to 0.09375
- up_w: bfloat16 [4096, 14336], P('dp', 'mp'), may hold values from -0.09375 to 0.09375
- cotangent: bfloat16 [3072, 14336], P('dp', 'mp'), may hold values from -6 to 6
Outputs:
- grad_gate: bfloat16 [4096, 14336], P('dp', 'mp')
- grad_up: bfloat16 [4096, 14336], P('dp', 'mp')
- hidden: bfloat16 [3072, 14336], P('dp', 'mp')
- cand_weight: float32 [4096], P('dp')
Inputs may be any that keep to these rules, and one draw needn't show every extreme that they name: `chosen`: all entries are distinct candidate indices. `counts`: exactly one training shard uses all 192 slots in every draw. `probe`: magnitudes at most 12 / sqrt(8192).
All inputs are finite; a program needn't handle non-finite values.
Results may differ from a plain program's by a relative error of at most 0.0057.
Values may be sent and summed in bfloat16 or wider, within the bound.
A program may use at most 128 MiB of HBM per device.

v0:
```python
import jax
import jax.numpy as jnp
from jax import lax
from jax.sharding import PartitionSpec as P


def gather_by_a2a(x, axis_name, axis):
    parts = lax.psum(1, axis_name)
    stacked = lax.all_to_all(
        jnp.broadcast_to(x[None], (parts,) + x.shape),
        axis_name,
        split_axis=0,
        concat_axis=0,
        tiled=True,
    )
    stacked = jnp.moveaxis(stacked, 0, axis)
    shape = list(x.shape)
    shape[axis] *= parts
    return stacked.reshape(shape)


def gather_rows(x):
    by_z = lax.all_gather(x, "z", axis=0)
    both = lax.all_gather(by_z, "core", axis=1)
    return both.reshape((-1,) + x.shape[1:])


def on_device(candidates, hold_gate, hold_up, probe, chosen, counts, gate_w, up_w, cotangent):
    cand_dev = candidates.shape[0]
    shards = chosen.shape[0]
    slots = chosen.shape[1]
    full_w = (gather_rows(gate_w), gather_rows(up_w))
    own_index = lax.axis_index("z") * lax.psum(1, "core") + lax.axis_index("core")
    source = chosen // cand_dev
    local_row = (chosen % cand_dev).reshape(-1)
    usable = (
        (jnp.arange(slots, dtype=jnp.int32)[None, :] < counts[:, None]) & (source == own_index)
    ).reshape(-1)
    onehot = (
        (local_row[:, None] == jnp.arange(cand_dev, dtype=jnp.int32)[None, :]) & usable[:, None]
    ).astype(jnp.bfloat16)
    picked = jnp.dot(onehot, candidates, preferred_element_type=jnp.float32).astype(jnp.bfloat16)
    picked = picked.reshape(shards, slots, candidates.shape[1])
    arrived = lax.all_to_all(picked, DP, split_axis=0, concat_axis=0, tiled=True)
    row_slab = jnp.sum(arrived.astype(jnp.float32), axis=0).astype(jnp.bfloat16)
    row_x = gather_by_a2a(row_slab, "mp", 1)
    row_slices = lax.all_to_all(row_x, DP, split_axis=1, concat_axis=0, tiled=True)
    incoming = gather_by_a2a(candidates, "mp", 1)
    hold_g = jnp.dot(incoming, hold_gate, preferred_element_type=jnp.float32)
    hold_u = jnp.dot(incoming, hold_up, preferred_element_type=jnp.float32)
    partial_score = jnp.sum(jax.nn.silu(hold_g) * hold_u * probe[None, :], axis=1)
    score = lax.psum(partial_score, "mp")
    cand_weight = jax.nn.sigmoid(score)
    picked_weight = (
        jnp.dot(
            onehot, cand_weight.astype(jnp.bfloat16)[:, None], preferred_element_type=jnp.float32
        )
        .astype(jnp.bfloat16)
        .reshape(shards, slots)
    )
    arrived_weight = lax.all_to_all(picked_weight, DP, split_axis=0, concat_axis=0, tiled=True)
    row_weight = jnp.sum(arrived_weight.astype(jnp.float32), axis=0)
    gate = jnp.dot(row_x, full_w[0], preferred_element_type=jnp.float32)
    up = jnp.dot(row_x, full_w[1], preferred_element_type=jnp.float32)
    hidden = (jax.nn.silu(gate) * up).astype(jnp.bfloat16)
    back = cotangent.astype(jnp.float32) * row_weight[:, None]
    sig = jax.nn.sigmoid(gate)
    d_up = (back * gate * sig).astype(jnp.bfloat16)
    d_gate = (back * up * sig * (1.0 + gate * (1.0 - sig))).astype(jnp.bfloat16)
    contract_rows = (((0,), (0,)), ((), ()))
    incoming = (gather_rows(d_gate), gather_rows(d_up))
    grad_g = lax.dot_general(
        row_slices, incoming[0], contract_rows, preferred_element_type=jnp.float32
    )
    grad_u = lax.dot_general(
        row_slices, incoming[1], contract_rows, preferred_element_type=jnp.float32
    )
    return (grad_g.astype(jnp.bfloat16), grad_u.astype(jnp.bfloat16), hidden, cand_weight)


DP = ("z", "core")


def solution(mesh):
    cores = 2
    mesh = jax.sharding.Mesh(
        mesh.devices.reshape(mesh.devices.shape[0] // cores, cores, mesh.devices.shape[1]),
        ("z", "core", "mp"),
    )
    placed = (
        P(DP, "mp"),
        P(None, "mp"),
        P(None, "mp"),
        P("mp"),
        P(),
        P(),
        P(DP, "mp"),
        P(DP, "mp"),
        P(DP, "mp"),
    )
    return jax.shard_map(
        on_device,
        mesh=mesh,
        in_specs=placed,
        out_specs=(P(DP, "mp"), P(DP, "mp"), P(DP, "mp"), P(DP)),
        check_vma=False,
    )
```

profile of v0, /device:TPU:1, one launch (start us, length us, event | category | flops | bytes accessed | tf_op | source)
XLA Modules:
  0.0 406.3 jit_solution(17809317110289626407)
XLA Ops:
  7.2 0.0 all-gather.21.cloned.1.call-start
  7.2 0.7 all-gather.21.cloned.1.call-update
  7.9 0.0 all-gather.17.cloned.1.call-start
  7.9 0.7 all-gather.17.cloned.1.call-update
  8.6 0.0 all-gather.23.cloned.1.call-start
  8.7 54.6 %all-gather.21.cloned.1.call-done = bf16[2048,896]{1,0:T(8,128)(2,1)} async-done(((bf16[256,896]{1,0:T(8,128)(2,1)}), bf16[2048,896]{1,0:T(8,128)(2,1)}) %all-gather.21.cloned.1.call-update) | async-done | bytes 3670032 | tf_op jit(solution)/shard_map/all_gather | solution.py:23
  63.3 0.0 copy-start.2
  63.3 0.0 all-gather.23.cloned.1.call-update
  63.3 0.0 all-gather.19.cloned.1.call-start
  63.3 50.2 %all-gather.17.cloned.1.call-done = bf16[2048,896]{1,0:T(8,128)(2,1)} async-done(((bf16[256,896]{1,0:T(8,128)(2,1)}), bf16[2048,896]{1,0:T(8,128)(2,1)}) %all-gather.17.cloned.1.call-update) | async-done | bytes 3670032 | tf_op jit(solution)/shard_map/all_gather | solution.py:23
  113.5 0.0 all-gather.19.cloned.1.call-update
  113.5 0.0 copy-done.2
  113.5 0.1 copy.16
  113.6 0.0 copy-start.3
  113.7 0.0 copy-start.4
  113.7 1.5 broadcast_in_dim.5
  115.2 6.5 %all-to-all-start.3 = ((bf16[16,256,256]{1,2,0:T(8,128)(2,1)}), bf16[16,256,256]{1,2,0:T(8,128)(2,1)S(1)}, u32[]{:S(2)}, u32[]{:S(2)}) async-start(bf16[16,256,256]{1,2,0:T(8,128)(2,1)} %broadcast_in_dim.5), calls=%async_computation.3 | async-start | bytes 4194304 | tf_op jit(solution)/shard_map/all_to_all | solution.py:9
  121.7 0.0 copy-done.3
  121.8 0.0 copy-done.4
  121.8 0.1 fusion.11
  121.8 0.1 and.28
  121.9 0.1 eq.23
  122.0 3.5 convolution_convert_fusion
  125.5 26.5 %all-to-all-done.3 = bf16[16,256,256]{1,2,0:T(8,128)(2,1)S(1)} async-done(((bf16[16,256,256]{1,2,0:T(8,128)(2,1)}), bf16[16,256,256]{1,2,0:T(8,128)(2,1)S(1)}, u32[]{:S(2)}, u32[]{:S(2)}) %all-to-all-start.3) | async-done | bytes 2097184 | tf_op jit(solution)/shard_map/all_to_all | solution.py:9
  152.0 0.0 copy-start
  152.0 1.3 copy-done
  153.3 6.6 %all-to-all-start = ((bf16[16,192,256]{2,1,0:T(8,128)(2,1)}), bf16[16,192,256]{2,1,0:T(8,128)(2,1)S(1)}, u32[]{:S(2)}, u32[]{:S(2)}) async-start(bf16[16,192,256]{2,1,0:T(8,128)(2,1)} %bitcast.41), calls=%async_computation | async-start | bytes 3145728 | tf_op jit(solution)/shard_map/all_to_all | solution.py:44
  159.9 0.0 copy-start.5
  159.9 0.0 copy-start.7
  159.9 4.3 %fusion.15 = f32[256,512]{1,0:T(8,128)S(1)} fusion(bf16[256,4096]{0,1:T(8,128)(2,1)} %bitcast.39, bf16[4096,512]{1,0:T(8,128)(2,1)} %param.10), kind=kOutput, calls=%fused_computation.32 | convolution fusion | flops 1073741824 | bytes 6815744 | tf_op jit(solution)/shard_map/dot_general | solution.py:49
  164.1 0.0 copy-done.1
  164.2 0.5 copy-done.5
  164.6 0.0 copy-done.7
  164.6 1.4 fusion.9
  166.0 31.8 %psum.7 = f32[256]{0:T(256)S(1)} all-reduce(f32[256]{0:T(256)S(1)} %fusion.9), channel_id=1, replica_groups=mesh['z'=8,'core'=2,'mp'=16] {'mp'}, use_global_device_ids=true, to_apply=%region_2.3 | all-reduce | flops 256 | bytes 2048 | tf_op jit(solution)/shard_map/psum | solution.py:52
  197.8 0.6 fusion.14
  198.4 2.5 fusion.1
  200.9 0.7 all_to_all.35
  201.6 0.0 all-to-all-done
  201.6 13.7 %all-to-all-start.4 = ((bf16[16,1,192]{2,1,0:T(2,128)(2,1)}), bf16[16,1,192]{2,1,0:T(2,128)(2,1)S(1)}, u32[]{:S(2)}, u32[]{:S(2)}) async-start(bf16[16,1,192]{2,1,0:T(2,128)(2,1)} %all_to_all.35), calls=%async_computation.4 | async-start | bytes 32768 | tf_op jit(solution)/shard_map/all_to_all | solution.py:61
  215.4 0.2 reduce_sum.30
  215.6 7.1 %all-to-all-done.4 = bf16[16,1,192]{2,1,0:T(2,128)(2,1)S(1)} async-done(((bf16[16,1,192]{2,1,0:T(2,128)(2,1)}), bf16[16,1,192]{2,1,0:T(2,128)(2,1)S(1)}, u32[]{:S(2)}, u32[]{:S(2)}) %all-to-all-start.4) | async-done | bytes 6176 | tf_op jit(solution)/shard_map/all_to_all | solution.py:61
  222.7 1.3 broadcast_in_dim.4
  224.0 3.7 all-to-all-start.1
  227.8 0.0 all-gather.29.cloned.1.call-start
  227.8 24.8 %all-to-all-done.1 = bf16[16,192,256]{2,1,0:T(8,128)(2,1)S(1)} async-done(((bf16[16,192,256]{2,1,0:T(8,128)(2,1)}), bf16[16,192,256]{2,1,0:T(8,128)(2,1)S(1)}, u32[]{:S(2)}, u32[]{:S(2)}) %all-to-all-start.1) | async-done | bytes 1572896 | tf_op jit(solution)/shard_map/all_to_all | solution.py:9
  252.7 0.2 copy.19
  252.8 0.0 all-gather.23.cloned.1.call-done
  252.9 0.0 copy-start.6
  252.9 5.8 %fusion.16 = f32[192,896]{1,0:T(8,128)} fusion(bf16[192,4096]{1,0:T(8,128)(2,1)S(1)} %bitcast.42, bf16[4096,896]{1,0:T(8,128)(2,1)} %bitcast.47), kind=kOutput, calls=%fused_computation.33 | convolution fusion | flops 1409286144 | bytes 9601024 | tf_op jit(solution)/shard_map/dot_general | solution.py:63
  258.7 0.0 copy-done.6
  258.7 6.1 %multiply_convert_fusion = (bf16[192,896]{1,0:T(8,128)(2,1)}, bf16[192,896]{1,0:T(8,128)(2,1)}, bf16[192,896]{1,0:T(8,128)(2,1)}) fusion(f32[192,896]{1,0:T(8,128)} %fusion.16, f32[192]{0:T(256)S(1)} %convert_reduce_fusion, bf16[192,896]{1,0:T(8,128)(2,1)S(1)} %copy-done.6, bf16[192,4096]{1,0:T(8,128)(2,1)S(1)} %bitcast.43, bf16[4096,896]{1,0:T(8,128)(2,1)} %bitcast.48), kind=kOutput, calls=%fused_computation.13 | convolution fusion | flops 1412382720 | bytes 10978048 | tf_op jit(solution)/shard_map/dot_general | solution.py:64
  264.9 0.0 all-gather.29.cloned.1.call-update
  264.9 0.0 all-gather.25.cloned.1.call-start
  264.9 0.5 all-gather.25.cloned.1.call-update
  265.5 0.0 all-gather.31.cloned.1.call-start
  265.5 32.7 %all-gather.29.cloned.1.call-done = bf16[1536,896]{1,0:T(8,128)(2,1)} async-done(((bf16[192,896]{1,0:T(8,128)(2,1)}), bf16[1536,896]{1,0:T(8,128)(2,1)}) %all-gather.29.cloned.1.call-update) | async-done | bytes 2752528 | tf_op jit(solution)/shard_map/all_gather | solution.py:23
  298.2 0.0 all-gather.31.cloned.1.call-update
  298.3 0.0 all-gather.27.cloned.1.call-start
  298.3 43.6 %all-gather.25.cloned.1.call-done = bf16[1536,896]{1,0:T(8,128)(2,1)} async-done(((bf16[192,896]{1,0:T(8,128)(2,1)}), bf16[1536,896]{1,0:T(8,128)(2,1)}) %all-gather.25.cloned.1.call-update) | async-done | bytes 2752528 | tf_op jit(solution)/shard_map/all_gather | solution.py:23
  341.9 0.0 all-gather.27.cloned.1.call-update
  341.9 47.2 %all_to_all.41 = bf16[192,16,256]{2,0,1:T(8,128)(2,1)S(1)} all-to-all(bf16[192,16,256]{2,0,1:T(8,128)(2,1)S(1)} %bitcast.34), channel_id=1, replica_groups=mesh['z'=8,'core'=2,'mp'=16] {'z','core'}, dimensions={1} | all-to-all | bytes 3145728 | tf_op jit(solution)/shard_map/all_to_all | solution.py:47
  389.1 5.2 %convolution_convert_fusion.1 = bf16[256,896]{1,0:T(8,128)(2,1)} fusion(bf16[3072,256]{1,0:T(8,128)(2,1)S(1)} %bitcast.44, bf16[3072,896]{1,0:T(8,128)(2,1)} %bitcast.49), kind=kOutput, calls=%fused_computation.8 | convolution fusion | flops 1409515520 | bytes 7536640 | tf_op jit(solution)/shard_map/dot_general | solution.py:75
  394.3 5.2 %convolution_convert_fusion.2 = bf16[256,896]{1,0:T(8,128)(2,1)} fusion(bf16[3072,256]{1,0:T(8,128)(2,1)S(1)} %bitcast.45, bf16[3072,896]{1,0:T(8,128)(2,1)} %bitcast.50), kind=kOutput, calls=%fused_computation.9 | convolution fusion | flops 1409515520 | bytes 7536640 | tf_op jit(solution)/shard_map/dot_general | solution.py:72
  (8 shorter events, 0.1 us)
Async XLA Ops:
  7.2 56.1 %all-gather.21.cloned.1.call-start = ((), (), s32[]{:S(2)}) async-start(), calls=%async_computation.7 | async-start | bytes 4128768 | tf_op jit(solution)/shard_map/all_gather | solution.py:23
  7.9 105.6 %all-gather.17.cloned.1.call-start = ((), (), s32[]{:S(2)}) async-start(), calls=%async_computation.5 | async-start | bytes 4128768 | tf_op jit(solution)/shard_map/all_gather | solution.py:23
  8.6 244.2 %all-gather.23.cloned.1.call-start = ((), (), s32[]{:S(2)}) async-start(), calls=%async_computation.8 | async-start | bytes 11010048 | tf_op jit(solution)/shard_map/all_gather | solution.py:24
  63.3 50.3 %copy-start.2 = (bf16[256,256]{1,0:T(8,128)(2,1)S(1)}, bf16[256,256]{1,0:T(8,128)(2,1)}, u32[]{:S(2)}) copy-start(bf16[256,256]{1,0:T(8,128)(2,1)} %param.9) | copy-start | bytes 393220
  63.3 195.5 %all-gather.19.cloned.1.call-start = ((), (), s32[]{:S(2)}) async-start(), calls=%async_computation.6 | async-start | bytes 11010048 | tf_op jit(solution)/shard_map/all_gather | solution.py:24
  113.6 8.1 %copy-start.3 = (s32[16,192]{1,0:T(8,128)S(1)}, s32[16,192]{1,0:T(8,128)}, u32[]{:S(2)}) copy-start(s32[16,192]{1,0:T(8,128)} %param.13) | copy-start | bytes 36868
  113.7 8.1 %copy-start.4 = (s32[16]{0:T(128)S(1)}, s32[16]{0:T(128)}, u32[]{:S(2)}) copy-start(s32[16]{0:T(128)} %param.14) | copy-start | bytes 196
  115.2 36.8 %all-to-all-start.3 = ((bf16[16,256,256]{1,2,0:T(8,128)(2,1)}), bf16[16,256,256]{1,2,0:T(8,128)(2,1)S(1)}, u32[]{:S(2)}, u32[]{:S(2)}) async-start(bf16[16,256,256]{1,2,0:T(8,128)(2,1)} %broadcast_in_dim.5), calls=%async_computation.3 | async-start | bytes 4194304 | tf_op jit(solution)/shard_map/all_to_all | solution.py:9
  152.0 1.3 copy-start
  153.3 48.3 %all-to-all-start = ((bf16[16,192,256]{2,1,0:T(8,128)(2,1)}), bf16[16,192,256]{2,1,0:T(8,128)(2,1)S(1)}, u32[]{:S(2)}, u32[]{:S(2)}) async-start(bf16[16,192,256]{2,1,0:T(8,128)(2,1)} %bitcast.41), calls=%async_computation | async-start | bytes 3145728 | tf_op jit(solution)/shard_map/all_to_all | solution.py:44
  159.9 4.3 %copy-start.1 = (bf16[16,256,256]{1,2,0:T(8,128)(2,1)S(1)}, bf16[16,256,256]{1,2,0:T(8,128)(2,1)}, u32[]{:S(2)}) copy-start(bf16[16,256,256]{1,2,0:T(8,128)(2,1)} %copy-done) | copy-start | bytes 6291460
  159.9 4.8 %copy-start.5 = (bf16[4096,512]{1,0:T(8,128)(2,1)S(1)}, bf16[4096,512]{1,0:T(8,128)(2,1)}, u32[]{:S(2)}) copy-start(bf16[4096,512]{1,0:T(8,128)(2,1)} %param.11) | copy-start | bytes 12582916
  159.9 4.8 %copy-start.7 = (f32[512]{0:T(512)S(1)}, f32[512]{0:T(512)}, u32[]{:S(2)}) copy-start(f32[512]{0:T(512)} %param.12) | copy-start | bytes 6148
  201.6 21.1 %all-to-all-start.4 = ((bf16[16,1,192]{2,1,0:T(2,128)(2,1)}), bf16[16,1,192]{2,1,0:T(2,128)(2,1)S(1)}, u32[]{:S(2)}, u32[]{:S(2)}) async-start(bf16[16,1,192]{2,1,0:T(2,128)(2,1)} %all_to_all.35), calls=%async_computation.4 | async-start | bytes 32768 | tf_op jit(solution)/shard_map/all_to_all | solution.py:61
  224.0 28.6 %all-to-all-start.1 = ((bf16[16,192,256]{2,1,0:T(8,128)(2,1)}), bf16[16,192,256]{2,1,0:T(8,128)(2,1)S(1)}, u32[]{:S(2)}, u32[]{:S(2)}) async-start(bf16[16,192,256]{2,1,0:T(8,128)(2,1)} %broadcast_in_dim.4), calls=%async_computation.1 | async-start | bytes 3145728 | tf_op jit(solution)/shard_map/all_to_all | solution.py:9
  227.8 70.5 %all-gather.29.cloned.1.call-start = ((), (), s32[]{:S(2)}) async-start(), calls=%async_computation.11 | async-start | bytes 3096576 | tf_op jit(solution)/shard_map/all_gather | solution.py:23
  252.9 5.9 %copy-start.6 = (bf16[192,896]{1,0:T(8,128)(2,1)S(1)}, bf16[192,896]{1,0:T(8,128)(2,1)}, u32[]{:S(2)}) copy-start(bf16[192,896]{1,0:T(8,128)(2,1)} %param.17) | copy-start | bytes 1032196
  264.9 77.0 %all-gather.25.cloned.1.call-start = ((), (), s32[]{:S(2)}) async-start(), calls=%async_computation.9 | async-start | bytes 3096576 | tf_op jit(solution)/shard_map/all_gather | solution.py:23
  265.5 123.6 %all-gather.31.cloned.1.call-start = ((), (), s32[]{:S(2)}) async-start(), calls=%async_computation.12 | async-start | bytes 8257536 | tf_op jit(solution)/shard_map/all_gather | solution.py:24
  298.3 96.0 %all-gather.27.cloned.1.call-start = ((), (), s32[]{:S(2)}) async-start(), calls=%async_computation.10 | async-start | bytes 8257536 | tf_op jit(solution)/shard_map/all_gather | solution.py:24
Sparse Core Ops, SparseCore 0:
  9.8 53.4 all-gather.20
  65.0 48.4 all-gather.16
  115.3 23.1 all-gather.22
  140.1 25.0 all-gather.18
  265.0 33.1 all-gather.28
  300.4 41.3 all-gather.24
  343.6 23.0 all-gather.30
  368.5 22.2 all-gather.26
where the time goes:
time: 407 us; the launch traced here: 406 us
  waiting for transfers between devices  241 us (59%)
  blocking collectives  79.1 us (19%)
  matrix products  33.9 us (8%)
  starting transfers between devices  30.9 us (8%)
  between operations  14.3 us (4%)
  local copies, waits for them, and re-layouts  5.83 us (1%)
    all_gather x4, waiting for transfers between devices, gather_rows(): by_z = lax.all_gather(x, 'z', axis=0)  181 us
    all_to_all x2, waiting for transfers between devices, gather_by_a2a(): lax.all_to_all(jnp.broadcast_to(x[None], (parts,) + x.shape), axis_name,...  51.3 us
    all_to_all x1, blocking collectives, on_device(): lax.all_to_all(row_x, DP, split_axis=1, concat_axis=0, tiled=True)  47.2 us
    psum x1, blocking collectives, on_device(): score = lax.psum(partial_score, 'mp')  31.8 us
    all_to_all x1, starting transfers between devices, on_device(): lax.all_to_all(picked_weight, DP, split_axis=0, concat_axis=0, tiled=True)  13.7 us
    all_to_all x2, starting transfers between devices, gather_by_a2a(): lax.all_to_all(jnp.broadcast_to(x[None], (parts,) + x.shape), axis_name,...  10.2 us
  transfers between devices with their start and end apart: 12, of which 7 were waited for; matrix products, arithmetic and copies ran while one was open for 7% of the time, Pallas kernels for 0%

commit v1 on v0

--- a/solution.py
+++ b/solution.py
@@ -49,7 +49,7 @@
     hold_g = jnp.dot(incoming, hold_gate, preferred_element_type=jnp.float32)
     hold_u = jnp.dot(incoming, hold_up, preferred_element_type=jnp.float32)
     partial_score = jnp.sum(jax.nn.silu(hold_g) * hold_u * probe[None, :], axis=1)
-    score = lax.psum(partial_score, "mp")
+    score = jnp.sum(lax.all_gather(partial_score, "mp"), 0)
     cand_weight = jax.nn.sigmoid(score)
     picked_weight = (
         jnp.dot(

time: 407 us -> 394 us (0.968)
  blocking collectives: 79.1 us -> 66.4 us
  waiting for transfers between devices: 241 us -> 251 us
  starting transfers between devices: 30.9 us -> 21.2 us
    psum x1 -> x0, blocking collectives: 31.8 us -> none  [on_device(): score = lax.psum(partial_score, 'mp')]
    all_gather x0 -> x1, blocking collectives: none -> 19.1 us  [on_device(): score = jnp.sum(lax.all_gather(partial_score, 'mp'), 0)]
    all_to_all x1, starting transfers between devices: 13.7 us -> 4.14 us  [on_device(): lax.all_to_all(picked_weight, DP, split_axis=0, concat_axis=0, tiled=True)]
    all_to_all x1, waiting for transfers between devices: 0.01 us -> 9.41 us  [on_device(): lax.all_to_all(picked, DP, split_axis=0, concat_axis=0, tiled=True)]
  transfers between devices with their start and end apart: 12 -> 12, of which waited for: 7 -> 8; matrix products, arithmetic and copies ran while one was open for 7% -> 7% of each run, Pallas kernels for 0% -> 0%
where the time goes in v1:
time: 394 us; the launch traced here: 393 us
  waiting for transfers between devices  251 us (64%)
  blocking collectives  66.4 us (17%)
  matrix products  33.9 us (9%)
  starting transfers between devices  21.2 us (5%)
  between operations  14.3 us (4%)
  local copies, waits for them, and re-layouts  5.83 us (1%)
    all_gather x4, waiting for transfers between devices, gather_rows(): by_z = lax.all_gather(x, 'z', axis=0)  181 us
    all_to_all x2, waiting for transfers between devices, gather_by_a2a(): lax.all_to_all(jnp.broadcast_to(x[None], (parts,) + x.shape), axis_name,...  51.3 us
    all_to_all x1, blocking collectives, on_device(): lax.all_to_all(row_x, DP, split_axis=1, concat_axis=0, tiled=True)  47.2 us
    all_gather x1, blocking collectives, on_device(): score = jnp.sum(lax.all_gather(partial_score, 'mp'), 0)  19.1 us
    all_to_all x2, starting transfers between devices, gather_by_a2a(): lax.all_to_all(jnp.broadcast_to(x[None], (parts,) + x.shape), axis_name,...  10.2 us
    all_to_all x1, waiting for transfers between devices, on_device(): lax.all_to_all(picked, DP, split_axis=0, concat_axis=0, tiled=True)  9.41 us
  transfers between devices with their start and end apart: 12, of which 8 were waited for; matrix products, arithmetic and copies ran while one was open for 7% of the time, Pallas kernels for 0%

profile of v1, /device:TPU:1, one launch (start us, length us, event | category | flops | bytes accessed | tf_op | source)
XLA Modules:
  0.0 393.4 jit_solution(1177093022415134326)
XLA Ops:
  7.2 0.0 all-gather.23.cloned.1.call-start
  7.2 0.7 all-gather.23.cloned.1.call-update
  7.9 0.0 all-gather.19.cloned.1.call-start
  7.9 0.7 all-gather.19.cloned.1.call-update
  8.6 0.0 all-gather.25.cloned.1.call-start
  8.7 54.6 %all-gather.23.cloned.1.call-done = bf16[2048,896]{1,0:T(8,128)(2,1)} async-done(((bf16[256,896]{1,0:T(8,128)(2,1)}), bf16[2048,896]{1,0:T(8,128)(2,1)}) %all-gather.23.cloned.1.call-update) | async-done | bytes 3670032 | tf_op jit(solution)/shard_map/all_gather | solution.py:23
  63.3 0.0 copy-start.2
  63.3 0.0 all-gather.25.cloned.1.call-update
  63.3 0.0 all-gather.21.cloned.1.call-start
  63.3 50.2 %all-gather.19.cloned.1.call-done = bf16[2048,896]{1,0:T(8,128)(2,1)} async-done(((bf16[256,896]{1,0:T(8,128)(2,1)}), bf16[2048,896]{1,0:T(8,128)(2,1)}) %all-gather.19.cloned.1.call-update) | async-done | bytes 3670032 | tf_op jit(solution)/shard_map/all_gather | solution.py:23
  113.5 0.0 all-gather.21.cloned.1.call-update
  113.5 0.0 copy-done.2
  113.5 0.1 copy.16
  113.6 0.0 copy-start.3
  113.7 0.0 copy-start.4
  113.7 1.5 broadcast_in_dim.5
  115.2 6.5 %all-to-all-start.3 = ((bf16[16,256,256]{1,2,0:T(8,128)(2,1)}), bf16[16,256,256]{1,2,0:T(8,128)(2,1)S(1)}, u32[]{:S(2)}, u32[]{:S(2)}) async-start(bf16[16,256,256]{1,2,0:T(8,128)(2,1)} %broadcast_in_dim.5), calls=%async_computation.3 | async-start | bytes 4194304 | tf_op jit(solution)/shard_map/all_to_all | solution.py:9
  121.7 0.0 copy-done.3
  121.8 0.0 copy-done.4
  121.8 0.1 fusion.11
  121.8 0.1 and.28
  121.9 0.1 eq.23
  122.0 3.5 convolution_convert_fusion
  125.5 26.5 %all-to-all-done.3 = bf16[16,256,256]{1,2,0:T(8,128)(2,1)S(1)} async-done(((bf16[16,256,256]{1,2,0:T(8,128)(2,1)}), bf16[16,256,256]{1,2,0:T(8,128)(2,1)S(1)}, u32[]{:S(2)}, u32[]{:S(2)}) %all-to-all-start.3) | async-done | bytes 2097184 | tf_op jit(solution)/shard_map/all_to_all | solution.py:9
  152.0 0.0 copy-start
  152.0 1.3 copy-done
  153.3 6.6 %all-to-all-start = ((bf16[16,192,256]{2,1,0:T(8,128)(2,1)}), bf16[16,192,256]{2,1,0:T(8,128)(2,1)S(1)}, u32[]{:S(2)}, u32[]{:S(2)}) async-start(bf16[16,192,256]{2,1,0:T(8,128)(2,1)} %bitcast.42), calls=%async_computation | async-start | bytes 3145728 | tf_op jit(solution)/shard_map/all_to_all | solution.py:44
  159.9 0.0 copy-start.5
  159.9 0.0 copy-start.7
  159.9 4.3 %fusion.15 = f32[256,512]{1,0:T(8,128)S(1)} fusion(bf16[256,4096]{0,1:T(8,128)(2,1)} %bitcast.40, bf16[4096,512]{1,0:T(8,128)(2,1)} %param.10), kind=kOutput, calls=%fused_computation.32 | convolution fusion | flops 1073741824 | bytes 6815744 | tf_op jit(solution)/shard_map/dot_general | solution.py:49
  164.1 0.0 copy-done.1
  164.2 0.5 copy-done.5
  164.6 0.0 copy-done.7
  164.6 1.4 fusion.9
  166.0 19.1 %all-gather.9 = f32[16,1,256]{2,1,0:T(1,128)S(1)} all-gather(f32[1,1,256]{2,1,0:T(1,128)S(1)} %bitcast.48), channel_id=2, replica_groups=mesh['z'=8,'core'=2,'mp'=16] {'mp'}, dimensions={0}, use_global_device_ids=true | all-gather | bytes 17408 | tf_op jit(solution)/shard_map/all_gather | solution.py:52
  185.2 0.6 fusion.14
  185.8 2.5 fusion.1
  188.3 0.7 all_to_all.35
  189.0 9.4 %all-to-all-done = bf16[16,192,256]{2,1,0:T(8,128)(2,1)S(1)} async-done(((bf16[16,192,256]{2,1,0:T(8,128)(2,1)}), bf16[16,192,256]{2,1,0:T(8,128)(2,1)S(1)}, u32[]{:S(2)}, u32[]{:S(2)}) %all-to-all-start) | async-done | bytes 1572896 | tf_op jit(solution)/shard_map/all_to_all | solution.py:44
  198.4 4.1 %all-to-all-start.4 = ((bf16[16,1,192]{2,1,0:T(2,128)(2,1)}), bf16[16,1,192]{2,1,0:T(2,128)(2,1)S(1)}, u32[]{:S(2)}, u32[]{:S(2)}) async-start(bf16[16,1,192]{2,1,0:T(2,128)(2,1)} %all_to_all.35), calls=%async_computation.4 | async-start | bytes 32768 | tf_op jit(solution)/shard_map/all_to_all | solution.py:61
  202.5 0.2 reduce_sum.39
  202.7 7.1 %all-to-all-done.4 = bf16[16,1,192]{2,1,0:T(2,128)(2,1)S(1)} async-done(((bf16[16,1,192]{2,1,0:T(2,128)(2,1)}), bf16[16,1,192]{2,1,0:T(2,128)(2,1)S(1)}, u32[]{:S(2)}, u32[]{:S(2)}) %all-to-all-start.4) | async-done | bytes 6176 | tf_op jit(solution)/shard_map/all_to_all | solution.py:61
  209.8 1.3 broadcast_in_dim.4
  211.2 3.7 all-to-all-start.1
  214.9 0.0 all-gather.31.cloned.1.call-start
  215.0 24.8 %all-to-all-done.1 = bf16[16,192,256]{2,1,0:T(8,128)(2,1)S(1)} async-done(((bf16[16,192,256]{2,1,0:T(8,128)(2,1)}), bf16[16,192,256]{2,1,0:T(8,128)(2,1)S(1)}, u32[]{:S(2)}, u32[]{:S(2)}) %all-to-all-start.1) | async-done | bytes 1572896 | tf_op jit(solution)/shard_map/all_to_all | solution.py:9
  239.8 0.2 copy.19
  240.0 0.0 all-gather.25.cloned.1.call-done
  240.0 0.0 copy-start.6
  240.0 5.8 %fusion.16 = f32[192,896]{1,0:T(8,128)} fusion(bf16[192,4096]{1,0:T(8,128)(2,1)S(1)} %bitcast.43, bf16[4096,896]{1,0:T(8,128)(2,1)} %bitcast.49), kind=kOutput, calls=%fused_computation.33 | convolution fusion | flops 1409286144 | bytes 9601024 | tf_op jit(solution)/shard_map/dot_general | solution.py:63
  245.9 0.0 copy-done.6
  245.9 6.1 %multiply_convert_fusion = (bf16[192,896]{1,0:T(8,128)(2,1)}, bf16[192,896]{1,0:T(8,128)(2,1)}, bf16[192,896]{1,0:T(8,128)(2,1)}) fusion(f32[192,896]{1,0:T(8,128)} %fusion.16, f32[192]{0:T(256)S(1)} %convert_reduce_fusion, bf16[192,896]{1,0:T(8,128)(2,1)S(1)} %copy-done.6, bf16[192,4096]{1,0:T(8,128)(2,1)S(1)} %bitcast.44, bf16[4096,896]{1,0:T(8,128)(2,1)} %bitcast.50), kind=kOutput, calls=%fused_computation.13 | convolution fusion | flops 1412382720 | bytes 10978048 | tf_op jit(solution)/shard_map/dot_general | solution.py:64
  252.0 0.0 all-gather.31.cloned.1.call-update
  252.0 0.0 all-gather.27.cloned.1.call-start
  252.1 0.5 all-gather.27.cloned.1.call-update
  252.6 0.0 all-gather.33.cloned.1.call-start
  252.7 32.7 %all-gather.31.cloned.1.call-done = bf16[1536,896]{1,0:T(8,128)(2,1)} async-done(((bf16[192,896]{1,0:T(8,128)(2,1)}), bf16[1536,896]{1,0:T(8,128)(2,1)}) %all-gather.31.cloned.1.call-update) | async-done | bytes 2752528 | tf_op jit(solution)/shard_map/all_gather | solution.py:23
  285.4 0.0 all-gather.33.cloned.1.call-update
  285.4 0.0 all-gather.29.cloned.1.call-start
  285.4 43.6 %all-gather.27.cloned.1.call-done = bf16[1536,896]{1,0:T(8,128)(2,1)} async-done(((bf16[192,896]{1,0:T(8,128)(2,1)}), bf16[1536,896]{1,0:T(8,128)(2,1)}) %all-gather.27.cloned.1.call-update) | async-done | bytes 2752528 | tf_op jit(solution)/shard_map/all_gather | solution.py:23
  329.0 0.0 all-gather.29.cloned.1.call-update
  329.0 47.2 %all_to_all.41 = bf16[192,16,256]{2,0,1:T(8,128)(2,1)S(1)} all-to-all(bf16[192,16,256]{2,0,1:T(8,128)(2,1)S(1)} %bitcast.35), channel_id=1, replica_groups=mesh['z'=8,'core'=2,'mp'=16] {'z','core'}, dimensions={1} | all-to-all | bytes 3145728 | tf_op jit(solution)/shard_map/all_to_all | solution.py:47
  376.2 5.2 %convolution_convert_fusion.1 = bf16[256,896]{1,0:T(8,128)(2,1)} fusion(bf16[3072,256]{1,0:T(8,128)(2,1)S(1)} %bitcast.45, bf16[3072,896]{1,0:T(8,128)(2,1)} %bitcast.51), kind=kOutput, calls=%fused_computation.8 | convolution fusion | flops 1409515520 | bytes 7536640 | tf_op jit(solution)/shard_map/dot_general | solution.py:75
  381.4 5.2 %convolution_convert_fusion.2 = bf16[256,896]{1,0:T(8,128)(2,1)} fusion(bf16[3072,256]{1,0:T(8,128)(2,1)S(1)} %bitcast.46, bf16[3072,896]{1,0:T(8,128)(2,1)} %bitcast.52), kind=kOutput, calls=%fused_computation.9 | convolution fusion | flops 1409515520 | bytes 7536640 | tf_op jit(solution)/shard_map/dot_general | solution.py:72
  (9 shorter events, 0.1 us)
Async XLA Ops:
  7.2 56.1 %all-gather.23.cloned.1.call-start = ((), (), s32[]{:S(2)}) async-start(), calls=%async_computation.7 | async-start | bytes 4128768 | tf_op jit(solution)/shard_map/all_gather | solution.py:23
  7.9 105.6 %all-gather.19.cloned.1.call-start = ((), (), s32[]{:S(2)}) async-start(), calls=%async_computation.5 | async-start | bytes 4128768 | tf_op jit(solution)/shard_map/all_gather | solution.py:23
  8.6 231.4 %all-gather.25.cloned.1.call-start = ((), (), s32[]{:S(2)}) async-start(), calls=%async_computation.8 | async-start | bytes 11010048 | tf_op jit(solution)/shard_map/all_gather | solution.py:24
  63.3 50.3 %copy-start.2 = (bf16[256,256]{1,0:T(8,128)(2,1)S(1)}, bf16[256,256]{1,0:T(8,128)(2,1)}, u32[]{:S(2)}) copy-start(bf16[256,256]{1,0:T(8,128)(2,1)} %param.9) | copy-start | bytes 393220
  63.3 182.6 %all-gather.21.cloned.1.call-start = ((), (), s32[]{:S(2)}) async-start(), calls=%async_computation.6 | async-start | bytes 11010048 | tf_op jit(solution)/shard_map/all_gather | solution.py:24
  113.6 8.1 %copy-start.3 = (s32[16,192]{1,0:T(8,128)S(1)}, s32[16,192]{1,0:T(8,128)}, u32[]{:S(2)}) copy-start(s32[16,192]{1,0:T(8,128)} %param.13) | copy-start | bytes 36868
  113.7 8.1 %copy-start.4 = (s32[16]{0:T(128)S(1)}, s32[16]{0:T(128)}, u32[]{:S(2)}) copy-start(s32[16]{0:T(128)} %param.14) | copy-start | bytes 196
  115.2 36.8 %all-to-all-start.3 = ((bf16[16,256,256]{1,2,0:T(8,128)(2,1)}), bf16[16,256,256]{1,2,0:T(8,128)(2,1)S(1)}, u32[]{:S(2)}, u32[]{:S(2)}) async-start(bf16[16,256,256]{1,2,0:T(8,128)(2,1)} %broadcast_in_dim.5), calls=%async_computation.3 | async-start | bytes 4194304 | tf_op jit(solution)/shard_map/all_to_all | solution.py:9
  152.0 1.3 copy-start
  153.3 45.1 %all-to-all-start = ((bf16[16,192,256]{2,1,0:T(8,128)(2,1)}), bf16[16,192,256]{2,1,0:T(8,128)(2,1)S(1)}, u32[]{:S(2)}, u32[]{:S(2)}) async-start(bf16[16,192,256]{2,1,0:T(8,128)(2,1)} %bitcast.42), calls=%async_computation | async-start | bytes 3145728 | tf_op jit(solution)/shard_map/all_to_all | solution.py:44
  159.9 4.3 %copy-start.1 = (bf16[16,256,256]{1,2,0:T(8,128)(2,1)S(1)}, bf16[16,256,256]{1,2,0:T(8,128)(2,1)}, u32[]{:S(2)}) copy-start(bf16[16,256,256]{1,2,0:T(8,128)(2,1)} %copy-done) | copy-start | bytes 6291460
  159.9 4.8 %copy-start.5 = (bf16[4096,512]{1,0:T(8,128)(2,1)S(1)}, bf16[4096,512]{1,0:T(8,128)(2,1)}, u32[]{:S(2)}) copy-start(bf16[4096,512]{1,0:T(8,128)(2,1)} %param.11) | copy-start | bytes 12582916
  159.9 4.8 %copy-start.7 = (f32[512]{0:T(512)S(1)}, f32[512]{0:T(512)}, u32[]{:S(2)}) copy-start(f32[512]{0:T(512)} %param.12) | copy-start | bytes 6148
  198.4 11.5 %all-to-all-start.4 = ((bf16[16,1,192]{2,1,0:T(2,128)(2,1)}), bf16[16,1,192]{2,1,0:T(2,128)(2,1)S(1)}, u32[]{:S(2)}, u32[]{:S(2)}) async-start(bf16[16,1,192]{2,1,0:T(2,128)(2,1)} %all_to_all.35), calls=%async_computation.4 | async-start | bytes 32768 | tf_op jit(solution)/shard_map/all_to_all | solution.py:61
  211.2 28.6 %all-to-all-start.1 = ((bf16[16,192,256]{2,1,0:T(8,128)(2,1)}), bf16[16,192,256]{2,1,0:T(8,128)(2,1)S(1)}, u32[]{:S(2)}, u32[]{:S(2)}) async-start(bf16[16,192,256]{2,1,0:T(8,128)(2,1)} %broadcast_in_dim.4), calls=%async_computation.1 | async-start | bytes 3145728 | tf_op jit(solution)/shard_map/all_to_all | solution.py:9
  214.9 70.5 %all-gather.31.cloned.1.call-start = ((), (), s32[]{:S(2)}) async-start(), calls=%async_computation.11 | async-start | bytes 3096576 | tf_op jit(solution)/shard_map/all_gather | solution.py:23
  240.0 5.9 %copy-start.6 = (bf16[192,896]{1,0:T(8,128)(2,1)S(1)}, bf16[192,896]{1,0:T(8,128)(2,1)}, u32[]{:S(2)}) copy-start(bf16[192,896]{1,0:T(8,128)(2,1)} %param.17) | copy-start | bytes 1032196
  252.0 76.9 %all-gather.27.cloned.1.call-start = ((), (), s32[]{:S(2)}) async-start(), calls=%async_computation.9 | async-start | bytes 3096576 | tf_op jit(solution)/shard_map/all_gather | solution.py:23
  252.6 123.6 %all-gather.33.cloned.1.call-start = ((), (), s32[]{:S(2)}) async-start(), calls=%async_computation.12 | async-start | bytes 8257536 | tf_op jit(solution)/shard_map/all_gather | solution.py:24
  285.4 96.0 %all-gather.29.cloned.1.call-start = ((), (), s32[]{:S(2)}) async-start(), calls=%async_computation.10 | async-start | bytes 8257536 | tf_op jit(solution)/shard_map/all_gather | solution.py:24
Sparse Core Ops, SparseCore 0:
  9.8 53.4 all-gather.22
  65.0 48.4 all-gather.18
  115.3 23.1 all-gather.24
  140.1 25.0 all-gather.20
  252.2 33.1 all-gather.30
  287.6 41.3 all-gather.26
  330.8 23.0 all-gather.32
  355.6 22.2 all-gather.28
